TPU v7x, 32 devices: a whole 2x2x4 slice. The times are simulated.
32 devices in a mesh: dp: 4 (over y, x), ctx: 8 (over z, core).
Axes of the slice: x: 2, y: 2, z: 4, core: 2. Of those that a mesh axis runs over, the one named last changes fastest.
Arguments:
- inputs: bfloat16 [8, 2048, 768], P('dp', 'ctx'), may hold values from -6 to 6
- segments: int32 [8, 2048], P('dp', 'ctx'), may hold values from 0 to 7, never falling along the last dimension, each value on 1 to 1024 neighbouring positions
- w_qkv: bfloat16 [768, 2304], P(('dp', 'ctx')), may hold values from -0.21875 to 0.21875
- b_query: bfloat16 [768], P(('dp', 'ctx')), may hold values from -3 to 3
- b_value: bfloat16 [768], P(('dp', 'ctx')), may hold values from -1.75 to 1.75
- w_out: bfloat16 [768, 768], P(('dp', 'ctx')), may hold values from -2.5 to 2.5
- b_attn: bfloat16 [768], P(('dp', 'ctx')), may hold values from -1.75 to 1.75
- gain_one: bfloat16 [768], P(('dp', 'ctx')), may hold values from 0.5 to 1.5
- shift_one: bfloat16 [768], P(('dp', 'ctx')), may hold values from -1.75 to 1.75
- w_in: bfloat16 [768, 3072], P(('dp', 'ctx')), may hold values from -0.21875 to 0.21875
- b_in: bfloat16 [3072], P(('dp', 'ctx')), may hold values from -1.75 to 1.75
- w_back: bfloat16 [3072, 768], P(('dp', 'ctx')), may hold values from -0.109375 to 0.109375
- b_back: bfloat16 [768], P(('dp', 'ctx')), may hold values from -1.75 to 1.75
- gain_two: bfloat16 [768], P(('dp', 'ctx')), may hold values from 0.5 to 1.5
- shift_two: bfloat16 [768], P(('dp', 'ctx')), may hold values from -1.75 to 1.75
- cotangent: bfloat16 [8, 2048, 768], P('dp', 'ctx'), may hold values from -6 to 6
Outputs:
- output: bfloat16 [8, 2048, 768], P('dp', 'ctx')
- input_grad: float32 [8, 2048, 768], P('dp', 'ctx')
- grad_w_qkv: float32 [768, 2304], P(('dp', 'ctx'))
- grad_b_query: float32 [768], P(('dp', 'ctx'))
- grad_b_value: float32 [768], P(('dp', 'ctx'))
- grad_w_out: float32 [768, 768], P(('dp', 'ctx'))
- grad_b_attn: float32 [768], P(('dp', 'ctx'))
- grad_gain_one: float32 [768], P(('dp', 'ctx'))
- grad_shift_one: float32 [768], P(('dp', 'ctx'))
- grad_w_in: float32 [768, 3072], P(('dp', 'ctx'))
- grad_b_in: float32 [3072], P(('dp', 'ctx'))
- grad_w_back: float32 [3072, 768], P(('dp', 'ctx'))
- grad_b_back: float32 [768], P(('dp', 'ctx'))
- grad_gain_two: float32 [768], P(('dp', 'ctx'))
- grad_shift_two: float32 [768], P(('dp', 'ctx'))
Inputs may be any that keep to these rules, and one draw needn't show every extreme that they name: `segments`: within each sequence segment numbers never fall; every document has 1 to 1024 tokens, and one of them has exactly that many.
All inputs are finite; a program needn't handle non-finite values.
Results may differ from a plain program's by a relative error of at most 0.015.
Values may be sent and summed in bfloat16 or wider, within the bound.
A program may use at most 192 MiB of HBM per device.

v0:
```python
import functools
import jax
import jax.numpy as jnp
from jax import lax
from jax.experimental import pallas as pl
from jax.experimental.pallas import tpu as pltpu
from jax.sharding import PartitionSpec as P

HEADS = 12
HEAD_DIM = 64
layer_eps = 1e-12
MESH_ID = pl.DeviceIdType.MESH
BF = jnp.bfloat16
F32 = jnp.float32
VMEM_LIMIT = 64 * 1024 * 1024 - 65536
SCORE_SCALE = 0.125 * 1.4426950408889634
EXCLUDE = -1e30


def place():
    d = lax.axis_index("dp")
    t = lax.axis_index("ctx")
    z = t // 2
    c = t % 2
    dx = d + 1 - 2 * (d % 2)
    dy = (d + 2) % 4
    return d, t, z, c, dx, dy


def remote(src, dst, ss, rs, dev):
    return pltpu.make_async_remote_copy(
        src_ref=src, dst_ref=dst, send_sem=ss, recv_sem=rs, device_id=dev, device_id_type=MESH_ID
    )


def greet(devices):
    bar = pltpu.get_barrier_semaphore()
    for dev in devices:
        pl.semaphore_signal(bar, inc=1, device_id=dev, device_id_type=MESH_ID)
    pl.semaphore_wait(bar, len(devices))


QB = 256
KB = 256
NH = 3


def marks_of(ids_row):
    kinds = lax.broadcasted_iota(jnp.int32, (16, ids_row.shape[1]), 0).astype(F32)
    return kinds == ids_row


N_ARR = 7
WIDE = (0, 1, 2)
EARLY = (3, 4, 5, 6)
FIRST_X = (0, 1, 3)
FIRST_Y = (2, 4, 5, 6)


def window(i):
    return (i // 4) * (i % 4), 8 - (1 - i // 4) * (3 - i % 4)


def front_kernel(x, idb, wi, wo, wb, sm, wq,
                 xs, ids, gi, go, gb, fv, bi, att, qkv, o32, lse, wt,
                 gs, gq, ka, va, qa, sb,
                 loc, s_x, r_x, s_xf, s_xd, r_xd, s_z, r_z, s_up, s_dn, s_px, r_px, s_py, r_py, s_f, r_f,
                 s_c, r_c, s_e, r_e):
    d, t, z, c, dx, dy = place()
    h = z // 2
    zp = z + 1 - 2 * (z % 2)
    inner = (z + h) % 2 == 1
    dxy = (dx + 2) % 4
    z1, z2 = 2 - h, 3 * (1 - h)
    others = [zp, z1, z2]
    far = [z1, z2]
    me = lambda zz: (d, zz * 2 + c)
    core = (d, z * 2 + 1 - c)
    nx, ny = (dx, t), (dy, t)
    greet([(d, (t + k) % 8) for k in range(1, 8)] + [nx, ny])
    sends = []

    def go_(cp):
        cp.start()
        sends.append(cp)

    def got(ref, ss, rs, dev):
        remote(ref, ref, ss, rs, dev).wait_recv()

    per = wq.shape[2] // 6
    dst = [gi, go, gb, gs, gq.at[0], gq.at[1], gq.at[2]]

    def mine(a, zz):
        if a < 4:
            return (wi, wo, wb, sm)[a]
        return wq.at[:, :, pl.ds(pl.multiple_of((a - 4) * 2 * per + (zz % 2) * per, per), per)]

    half = x.shape[1] // 2

    def piece(k, hh, tt):
        if k == 2:
            return idb.at[hh], ids.at[tt]
        rows = pl.ds(k * half, half)
        return x.at[hh, rows], xs.at[tt, rows]

    for a in EARLY:
        for k in range(3):
            zz = others[k]
            go_(remote(mine(a, zz), dst[a].at[d, z, c], s_z.at[a - 3, k], r_z.at[a, z], me(zz)))

    def plane(arrs, zz, first):
        for a in arrs:
            src = mine(a, z) if first else dst[a].at[d, zz, c]
            go_(remote(src, dst[a].at[d, zz, c], s_px.at[a, zz], r_px.at[a, zz], nx))
            go_(remote(src, dst[a].at[d, zz, c], s_py.at[a, zz], r_py.at[a, zz], ny))

    plane(EARLY, z, True)
    for k in (2, 0, 1):
        src, to = piece(k, 1 - h, t)
        go_(remote(src, to, s_x.at[0, k], r_x.at[z, k], me(z1)))
        src, to = piece(k, h, t)
        go_(remote(src, to, s_x.at[1, k], r_x.at[z, k], me(zp)))

    def chain(zz, first, wait):
        for a in WIDE:
            src = mine(a, z) if first else dst[a].at[d, zz, c]
            up = remote(src, dst[a].at[d, zz, c], s_up.at[a, zz], r_z.at[a, zz], me((z + 1) % 4))
            dn = remote(src, dst[a].at[d, zz, c], s_dn.at[a, zz], r_z.at[a, zz], me((z + 3) % 4))

            @pl.when(jnp.logical_and(zz <= z, z < 3))
            def _(up=up):
                if wait:
                    up.wait_send()
                else:
                    up.start()

            @pl.when(jnp.logical_and(zz >= z, z > 0))
            def _(dn=dn):
                if wait:
                    dn.wait_send()
                else:
                    dn.start()

    chain(z, True, False)
    plane(WIDE, z, True)
    locals_ = [pltpu.make_async_copy(piece(k, h, t)[0], piece(k, h, t)[1], loc.at[N_ARR + k]) for k in range(3)]
    for a in (4, 5, 6, 3, 0, 1, 2):
        locals_.append(pltpu.make_async_copy(mine(a, z), dst[a].at[d, z, c], loc.at[a]))
    for cp in locals_:
        cp.start()

    def forward(arrs, zz):
        for a in arrs:
            if a in FIRST_Y:
                got(dst[a].at[dy, zz, c], s_py.at[a, zz], r_py.at[a, zz], ny)
                go_(remote(dst[a].at[dy, zz, c], dst[a].at[dy, zz, c], s_f.at[a, zz], r_f.at[a, zz], nx))
            else:
                got(dst[a].at[dx, zz, c], s_px.at[a, zz], r_px.at[a, zz], nx)
                go_(remote(dst[a].at[dx, zz, c], dst[a].at[dx, zz, c], s_f.at[a, zz], r_f.at[a, zz], ny))

    def across(arrs, zz):
        for a in arrs:
            if a in FIRST_Y:
                got(dst[a].at[dx, zz, c], s_px.at[a, zz], r_px.at[a, zz], nx)
                got(dst[a].at[dxy, zz, c], s_f.at[a, zz], r_f.at[a, zz], nx)
            else:
                got(dst[a].at[dy, zz, c], s_py.at[a, zz], r_py.at[a, zz], ny)
                got(dst[a].at[dxy, zz, c], s_f.at[a, zz], r_f.at[a, zz], ny)
            go_(remote(dst[a].at[:, zz, c], dst[a].at[:, zz, c], s_c.at[a, zz], r_c.at[a, zz], core))

    def crossed(arrs, zz):
        for a in arrs:
            ref = dst[a].at[:, zz, 1 - c]
            got(ref, s_c.at[a, zz], r_c.at[a, zz], core)

    def arrive(arrs, k):
        for a in arrs:
            got(dst[a].at[d, others[k], c], s_z.at[0, 0], r_z.at[a, others[k]], me(others[k]))

    for k in range(3):
        arrive(EARLY, k)
        plane(EARLY, others[k], False)
    for cp in locals_[:7]:
        cp.wait()
    for zz in [z] + others:
        forward(EARLY, zz)

    def relay(k, wait):
        for j in range(2):
            ref = piece(k, h, far[j] * 2 + c)[1]
            cp = remote(ref, ref, s_xf.at[j, k], r_x.at[far[j], k], me(zp))

            @pl.when(inner)
            def _(cp=cp):
                if wait:
                    cp.wait_send()
                else:
                    cp.wait_recv()
                    cp.start()

    def relayed(k):
        for j in range(2):
            ref = piece(k, h, far[j] * 2 + c)[1]

            @pl.when(jnp.logical_not(inner))
            def _(ref=ref, j=j):
                got(ref, s_x.at[0, k], r_x.at[far[j], k], me(zp))

    def to_core(zz):
        for k in range(3):
            ref = piece(k, h, zz * 2 + c)[1]
            go_(remote(ref, ref, s_xd.at[zz, k], r_xd.at[zz, k], core))

    def from_core(zz):
        for k in range(3):
            got(piece(k, h, zz * 2 + 1 - c)[1], s_xd.at[zz, k], r_xd.at[zz, k], core)

    to_core(z)
    for k in (2, 0):
        relay(k, False)
    for zz in [z] + others:
        across(EARLY, zz)
    relay(1, False)
    for k in range(3):
        got(piece(k, h, zp * 2 + c)[1], s_x.at[1, k], r_x.at[zp, k], me(zp))
    to_core(zp)
    for zz in [z] + others:
        crossed(EARLY, zz)
    width = wt.shape[3]
    for j in range(3):
        for q in range(2):
            w = gq[j, 2 * q:2 * q + 2].astype(F32).reshape(width // 2, per)
            w = w.T.astype(BF)
            for cc in range(2):
                wt[j, cc, :, q * (width // 2):(q + 1) * (width // 2)] = w[cc * (per // 2):(cc + 1) * (per // 2)]
    group = (z % 2) * 2 + c
    span = x.shape[1]

    def column(row):
        v = gs[group, :, :, row].reshape(8, 128).T
        return jnp.concatenate([v[:24, r:r + 1] for r in range(8)], axis=0)

    bias = [column(0), None, column(1)]
    for g in range(NH):
        va[g, 64:] = jnp.ones((16, va.shape[2]), BF)

    def project(zz):
        def one(j, _):
            tb = zz * 2 + j
            cols = pl.ds(pl.multiple_of(tb * span, span), span)
            xb = xs[tb]
            hit = marks_of(ids[tb, 0:1])
            ones = jnp.where(hit, 1.0, 0.0)
            away = jnp.where(hit, 0.0, EXCLUDE).astype(BF)
            for s in range(3):
                r = lax.dot_general(wt[s, c], xb, (((1,), (1,)), ((), ())), preferred_element_type=F32)
                if bias[s] is not None:
                    r = r + bias[s]
                low = r.astype(BF)
                qkv[s, :, cols] = low
                for g in range(NH):
                    part = low[g * 64:(g + 1) * 64]
                    if s == 0:
                        qa[g, :64, cols] = part
                        qa[g, 64:, cols] = away
                    elif s == 1:
                        ka[g, cols, :] = jnp.concatenate([part.astype(F32), ones], axis=0).T.astype(BF)
                    else:
                        va[g, :64, cols] = part
            return 0

        lax.fori_loop(0, 2, one, 0)

    forward(WIDE, z)
    for zz in (z, zp):
        from_core(zz)
        project(zz)
    for k in (2, 0, 1):
        relayed(k)
    for zz in far:
        to_core(zz)
    for zz in far:
        from_core(zz)
        project(zz)

    def attend(k):
        i = (t + k) % 8
        cols = pl.ds(pl.multiple_of(i * QB, QB), QB)
        lo, hi = window(i)

        def block(j, carry):
            at = pl.ds(pl.multiple_of(j * KB, KB), KB)
            out = []
            s = [jnp.dot(ka[g, at, :], qa[g, :, cols], preferred_element_type=F32) for g in range(NH)]
            for g in range(NH):
                m, acc = carry[g]
                m2 = jnp.maximum(m, jnp.max(s[g], axis=0, keepdims=True))
                p = jnp.exp2((s[g] - m2) * SCORE_SCALE).astype(BF)
                acc = acc * jnp.exp2((m - m2) * SCORE_SCALE) + jnp.dot(
                    va[g, :, at], p, preferred_element_type=F32)
                out.append((m2, acc))
            return tuple(out)

        first = tuple((jnp.full((1, QB), -3e38, F32), jnp.zeros((80, QB), F32)) for _ in range(NH))
        res = lax.fori_loop(lo, hi, block, first)
        for g in range(NH):
            m, acc = res[g]
            total = acc[64:65]
            o = acc[:64] / total
            o32[i, g * 64:(g + 1) * 64] = o
            if k:
                sb[i, g * 64:(g + 1) * 64] = o.astype(BF)
            else:
                att[t, g * 64:(g + 1) * 64] = o.astype(BF)
            lse[g, pl.ds(i, 1)] = m * SCORE_SCALE + jnp.log2(total)
        if k:
            go_(remote(sb.at[i], att.at[t], s_e.at[k - 1], r_e.at[k - 1], (d, i)))

    def onward(k):
        arrive(WIDE, k)
        chain(others[k], False, False)
        plane(WIDE, others[k], False)

    order = ORDER_K
    attend(order[0])
    onward(0)
    attend(order[1])
    for cp in locals_[7:]:
        cp.wait()
    across(WIDE, z)
    attend(order[2])
    onward(1)
    attend(order[3])
    forward(WIDE, zp)
    attend(order[4])
    onward(2)
    attend(order[5])
    forward(WIDE, z1)
    across(WIDE, zp)
    attend(order[6])
    attend(order[7])
    forward(WIDE, z2)
    across(WIDE, z1)
    across(WIDE, z2)
    for r in range(32):
        v = gs.at[r // 8, (r // 2) % 4, r % 2]
        fv[:, 24 * r:24 * r + 24] = v[0:8, 0:24]
        bi[:, 96 * r:96 * r + 96] = v[8:9, 0:96]
    for zz in [z] + others:
        crossed(WIDE, zz)
    for k in range(1, 8):
        src = (t + 8 - k) % 8
        got(att.at[src], s_e.at[k - 1], r_e.at[k - 1], (d, src))
    for cp in sends:
        cp.wait_send()
    chain(z, True, True)
    for zz in others:
        chain(zz, False, True)
    for k in range(3):
        relay(k, True)


ORDER_K = (4, 3, 5, 2, 6, 1, 7, 0)


def any_spec():
    return pl.BlockSpec(memory_space=pl.ANY)


def vmem_spec():
    return pl.BlockSpec(memory_space=pltpu.VMEM)


def dma(*shape):
    return pltpu.SemaphoreType.DMA(shape)


def front(x, idb, wi, wo, wb, sm, wq):
    span, width = x.shape[1:]
    n = 8 * span
    per = width // 4
    grid_of = lambda a: jax.ShapeDtypeStruct((4, 4, 2) + a.shape, a.dtype)
    return pl.pallas_call(
        front_kernel,
        out_shape=[
            jax.ShapeDtypeStruct((8, span, width), x.dtype),
            jax.ShapeDtypeStruct((8, 8, span), F32),
            grid_of(wi), grid_of(wo), grid_of(wb),
            jax.ShapeDtypeStruct((8, width), F32), jax.ShapeDtypeStruct((1, wi.shape[2]), F32),
            jax.ShapeDtypeStruct((8, per, span), BF),
            jax.ShapeDtypeStruct((3, per, n), BF),
            jax.ShapeDtypeStruct((8, per, span), F32),
            jax.ShapeDtypeStruct((NH, 8, span), F32),
            jax.ShapeDtypeStruct((3, 2, per, width), BF),
        ],
        in_specs=[any_spec()] * 7,
        out_specs=[vmem_spec()] * 2 + [any_spec()] * 3 + [vmem_spec()] * 7,
        scratch_shapes=[
            pltpu.VMEM((4, 4, 2) + sm.shape, F32),
            pltpu.VMEM((3, 4, 4, 2) + wq.shape[:2] + (2 * per,), BF),
            pltpu.VMEM((NH, n, 80), BF), pltpu.VMEM((NH, 80, n), BF), pltpu.VMEM((NH, 80, n), BF),
            pltpu.VMEM((8, per, span), BF),
            dma(N_ARR + 3), dma(2, 3), dma(4, 3), dma(2, 3), dma(4, 3), dma(4, 3), dma(4, 3), dma(N_ARR, 4),
            dma(3, 4), dma(3, 4),
            dma(N_ARR, 4), dma(N_ARR, 4), dma(N_ARR, 4), dma(N_ARR, 4), dma(N_ARR, 4), dma(N_ARR, 4),
            dma(N_ARR, 4), dma(N_ARR, 4), dma(7), dma(7),
        ],
        compiler_params=pltpu.CompilerParams(
            collective_id=1, has_side_effects=True, vmem_limit_bytes=VMEM_LIMIT),
        name="front",
    )(x, idb, wi, wo, wb, sm, wq)


def back_kernel(dat, di, do_, db, ds_, qkv, ids, o32, lse, wt, xs, d_one,
                ox, oi, oo, ob, os_, oq, ov, *rest):
    rd, own, r1, r2, r3, r4, r5 = [rest[4 * i:4 * i + 4] for i in range(7)]
    (da, ka, qa, vk, dkv, pr, xv, dxp, dw, lq, lv,
     xd, x3, x4, x5, q0, q1, q2, qr, v0, v1, v2, vr,
     loc, s_e, r_e, s_d, r_d, s_1, r_1, s_2, r_2, s_3, r_3, s_4, r_4, s_5, r_5,
     s_q1, r_q1, s_q2, r_q2, s_qe, r_qe) = rest[28:]
    d, t, z, c, dx, dy = place()
    x, y = d % 2, d // 2
    h = z // 2
    zp = z + 1 - 2 * (z % 2)
    inner = (z + h) % 2 == 1
    me = lambda zz: (d, zz * 2 + c)
    core = (d, z * 2 + 1 - c)
    nx, ny = (dx, t), (dy, t)
    line = [(t + k) % 8 for k in range(1, 8)]
    far = [2 * (1 - h), 2 * (1 - h) + 1]
    order = [far[0], far[1], zp, z]
    group = (z % 2) * 2 + c
    part = [di, do_, db, ds_]
    outs = [oi, oo, ob, os_]
    by_x = [True, True, False, True]
    sends = []
    greet([(d, o) for o in line] + [nx, ny])

    def go_(cp):
        cp.start()
        sends.append(cp)

    def got(ref, ss, rs, dev):
        remote(ref, ref, ss, rs, dev).wait_recv()

    for k in NEAR[1:]:
        i = line[k - 1]
        go_(remote(dat.at[i], da.at[t], s_e.at[k - 1], r_e.at[k - 1], (d, i)))
    for n_, zz in enumerate(order):
        for a in range(4):
            for yy in range(2):
                go_(remote(part[a].at[yy, :, zz, 1 - c], rd[a].at[yy, :, zz], s_d.at[1 + 2 * a + yy, n_],
                           r_d.at[1 + 2 * a + yy, n_], core))
    local = []

    def here(src, to):
        cp = pltpu.make_async_copy(src, to, loc.at[len(local)])
        cp.start()
        local.append(cp)

    here(dat.at[t], da.at[t])
    for a in range(4):
        for yy in range(2):
            here(part[a].at[yy, :, :, c], own[a].at[yy])
    here(xs, xv)

    n = qkv.shape[2]
    span = da.shape[2]

    def fill(tb, _):
        cols = pl.ds(pl.multiple_of(tb * span, span), span)
        hit = marks_of(ids[tb, 0:1])
        ones = jnp.where(hit, 1.0, 0.0)
        away = jnp.where(hit, 0.0, EXCLUDE).astype(BF)
        for g in range(NH):
            rows = slice(g * 64, (g + 1) * 64)
            ka[g, cols, :] = jnp.concatenate([qkv[1, rows, cols].astype(F32), ones], axis=0).T.astype(BF)
            vk[g, cols, :] = qkv[2, rows, cols].astype(F32).T.astype(BF)
            qa[g, :64, cols] = qkv[0, rows, cols]
            qa[g, 64:, cols] = away
            dkv[g, cols, :] = jnp.zeros((span, 128), F32)
        return 0

    lax.fori_loop(0, 8, fill, 0)

    def attend(k):
        i = (t + 8 - k) % 8
        if k:
            got(da.at[i], s_e.at[k - 1], r_e.at[k - 1], (d, i))
        cols = pl.ds(pl.multiple_of(i * QB, QB), QB)
        lo, hi = window(i)
        fixed = []
        for g in range(NH):
            rows = slice(g * 64, (g + 1) * 64)
            do = da[i, rows].astype(F32)
            inside = jnp.sum(do * o32[i, rows], axis=0, keepdims=True)
            zero = jnp.zeros((64, QB), F32)
            ra = jnp.concatenate([do, zero], axis=0).T.astype(BF)
            rb = jnp.concatenate([zero, qkv[0, rows, cols].astype(F32)], axis=0).T.astype(BF)
            fixed.append((inside, lse[g, pl.ds(i, 1)], ra, rb))

        def block(j, carry):
            at = pl.ds(pl.multiple_of(j * KB, KB), KB)
            out = []
            s = [jnp.dot(ka[g, at, :], qa[g, :, cols], preferred_element_type=F32) for g in range(NH)]
            dp = [jnp.dot(vk[g, at, :], da[i, g * 64:(g + 1) * 64], preferred_element_type=F32)
                  for g in range(NH)]
            for g in range(NH):
                inside, lse_i, ra, rb = fixed[g]
                p = jnp.exp2(s[g] * SCORE_SCALE - lse_i)
                ds = (p * (dp[g] - inside)).astype(BF)
                dkv[g, at, :] += jnp.dot(p.astype(BF), ra, preferred_element_type=F32) + jnp.dot(
                    ds, rb, preferred_element_type=F32)
                out.append(carry[g] + jnp.dot(qkv[1, g * 64:(g + 1) * 64, at], ds, preferred_element_type=F32))
            return tuple(out)

        dq = lax.fori_loop(lo, hi, block, tuple(jnp.zeros((64, QB), F32) for _ in range(NH)))
        for g in range(NH):
            pr[0, g * 64:(g + 1) * 64, cols] = (dq[g] * 0.125).astype(BF)

    def add_rows(dst, src):
        def step(i, _):
            dst[i] = dst[i] + src[i]
            return 0

        lax.fori_loop(0, dst.shape[0], step, 0)

    def add_tok(dst, src):
        def step(i, _):
            at = pl.ds(pl.multiple_of(i * 32, 32), 32)
            dst[at, :] = dst[at, :] + src[at, :]
            return 0

        lax.fori_loop(0, dst.shape[0] // 32, step, 0)

    def first(n_):
        zz = order[n_]
        for a in range(4):
            for yy in range(2):
                got(rd[a].at[yy, :, zz], s_d.at[1 + 2 * a + yy, n_], r_d.at[1 + 2 * a + yy, n_], core)
                for xx in range(2):
                    add_rows(rd[a].at[yy, xx, zz], own[a].at[yy, xx, zz])
            if by_x[a]:
                go_(remote(rd[a].at[:, 1 - x, zz], r1[a].at[n_], s_1.at[a, n_], r_1.at[a, n_], nx))
            else:
                go_(remote(rd[a].at[1 - y, :, zz], r1[a].at[n_], s_1.at[a, n_], r_1.at[a, n_], ny))

    def second(n_):
        zz = order[n_]
        for a in range(4):
            got(r1[a].at[n_], s_1.at[a, n_], r_1.at[a, n_], nx if by_x[a] else ny)
            for w in range(2):
                add_rows(rd[a].at[w, x, zz] if by_x[a] else rd[a].at[y, w, zz], r1[a].at[n_, w])
            if by_x[a]:
                go_(remote(rd[a].at[1 - y, x, zz], r2[a].at[n_], s_2.at[a, n_], r_2.at[a, n_], ny))
            else:
                go_(remote(rd[a].at[y, 1 - x, zz], r2[a].at[n_], s_2.at[a, n_], r_2.at[a, n_], nx))

    def to_inner(a, n_):
        ref = xd.at[far[n_]] if a == 4 else rd[a].at[y, x, far[n_]]
        land = x3 if a == 4 else r3[a]
        return remote(ref, land.at[n_], s_3.at[a, n_], r_3.at[a, n_], me(zp))

    def to_far(a, n_):
        ref = xd.at[far[n_]] if a == 4 else rd[a].at[y, x, far[n_]]
        return remote(ref, x4 if a == 4 else r4[a], s_4.at[a, n_], r_4.at[a], me(far[n_]))

    def third(n_):
        zz = order[n_]
        for a in range(4):
            got(r2[a].at[n_], s_2.at[a, n_], r_2.at[a, n_], ny if by_x[a] else nx)
            add_rows(rd[a].at[y, x, zz], r2[a].at[n_])
            if n_ < 2:
                @pl.when(jnp.logical_not(inner))
                def _(a=a):
                    to_inner(a, n_).start()
            elif n_ == 2:
                go_(remote(rd[a].at[y, x, zz], r5[a], s_5.at[a], r_5.at[a], me(zz)))

    def fourth(n_, arrs):
        @pl.when(inner)
        def _():
            for a in arrs:
                to_inner(a, n_).wait_recv()
                if a == 4:
                    add_tok(xd.at[far[n_]], x3.at[n_])
                else:
                    add_rows(rd[a].at[y, x, far[n_]], r3[a].at[n_])
                to_far(a, n_).start()

    for cp in local:
        cp.wait()
    first(0)
    first(1)
    attend(NEAR[0])
    attend(NEAR[1])
    second(0)
    first(2)
    attend(NEAR[2])
    attend(NEAR[3])
    second(1)
    first(3)
    attend(NEAR[4])
    third(0)
    attend(NEAR[5])
    second(2)
    attend(NEAR[6])
    third(1)
    fourth(0, range(4))
    attend(NEAR[7])
    second(3)
    for g in range(NH):
        rows = slice(g * 64, (g + 1) * 64)
        flip = dkv[g].T
        pr[1, rows] = (flip[64:] * 0.125).astype(BF)
        pr[2, rows] = flip[:64].astype(BF)

    def token_grad(tb):
        cols = pl.ds(pl.multiple_of(tb * span, span), span)
        acc = None
        for s in range(3):
            term = jnp.dot(pr[s, :, cols].astype(F32).T.astype(BF), wt[s, c], preferred_element_type=F32)
            acc = term if acc is None else acc + term
        dxp[tb] = acc.astype(BF)

    def token_pair(j, _):
        token_grad(j * 2 + 1 - c)
        return 0

    lax.fori_loop(0, 4, token_pair, 0)
    for n_, zz in enumerate(order):
        go_(remote(dxp.at[zz * 2 + 1 - c], xd.at[zz], s_d.at[0, n_], r_d.at[0, n_], core))
    third(2)
    fourth(1, range(4))

    def token_mine(j, _):
        token_grad(j * 2 + c)
        return 0

    lax.fori_loop(0, 4, token_mine, 0)
    for n_, zz in enumerate(order):
        got(xd.at[zz], s_d.at[0, n_], r_d.at[0, n_], core)
        add_tok(xd.at[zz], dxp.at[zz * 2 + c])
        if n_ < 2:
            @pl.when(jnp.logical_not(inner))
            def _(n_=n_):
                to_inner(4, n_).start()
        elif n_ == 2:
            go_(remote(xd.at[zz], x5, s_5.at[4], r_5.at[4], me(zz)))
    per = pr.shape[1]
    width = wt.shape[3]
    xall = xv[...].reshape(n, width)
    for s in range(3):
        dw[s * per:(s + 1) * per] = jnp.dot(pr[s], xall, preferred_element_type=F32)
    for q in range(2):
        w = dw[:, q * (width // 2):(q + 1) * (width // 2)].T
        lq[q] = w.reshape(lq.shape[1:]).astype(BF)
    lv[...] = jnp.zeros_like(lv)
    for row, s in ((0, 0), (1, 2)):
        col = jnp.sum(pr[s].astype(F32), axis=1, keepdims=True)
        for r in range(8):
            piece = jnp.broadcast_to(col[24 * r:24 * r + 24], (24, 128)).T
            lv[group // 2, group % 2, r // 2, r % 2, row:row + 1, :24] = piece[0:1]
    lq_x = lq
    go_(remote(lq_x.at[:, 1 - x], q1, s_q1.at[0], r_q1.at[0], nx))
    go_(remote(lv.at[:, 1 - x], v1, s_q1.at[1], r_q1.at[1], nx))
    third(3)
    fourth(0, (4,))
    fourth(1, (4,))
    got(q1, s_q1.at[0], r_q1.at[0], nx)
    got(v1, s_q1.at[1], r_q1.at[1], nx)
    for yy in range(2):
        for zc in range(8):
            at = (zc // 2, zc % 2)
            q0[(yy,) + at] = q1[(yy,) + at] + lq[(yy, x) + at]
            v0[(yy,) + at] = v1[(yy,) + at] + lv[(yy, x) + at]
    go_(remote(q0.at[1 - y], q2, s_q2.at[0], r_q2.at[0], ny))
    go_(remote(v0.at[1 - y], v2, s_q2.at[1], r_q2.at[1], ny))
    src_in = 2 - h
    for a in range(4):
        got(r5[a], s_5.at[a], r_5.at[a], me(zp))
        got(r4[a], s_4.at[a, 0], r_4.at[a], me(src_in))
        acc = rd[a].at[y, x, z]
        for i in range(acc.shape[0]):
            outs[a][i] = acc[i].astype(F32) + r5[a][i].astype(F32) + r4[a][i].astype(F32)
    got(q2, s_q2.at[0], r_q2.at[0], ny)
    got(v2, s_q2.at[1], r_q2.at[1], ny)
    for zc in range(8):
        at = (zc // 2, zc % 2)
        q0[(y,) + at] = q0[(y,) + at] + q2[at]
        v0[(y,) + at] = v0[(y,) + at] + v2[at]
    for k in range(1, 8):
        to = line[k - 1]
        go_(remote(q0.at[y, to // 2, to % 2], qr.at[t], s_qe.at[0, k - 1], r_qe.at[0, k - 1], (d, to)))
        go_(remote(v0.at[y, to // 2, to % 2], vr.at[t], s_qe.at[1, k - 1], r_qe.at[1, k - 1], (d, to)))
    qr[t] = q0[y, z, c]
    vr[t] = v0[y, z, c]
    got(x5, s_5.at[4], r_5.at[4], me(zp))
    got(x4, s_4.at[4, 0], r_4.at[4], me(src_in))

    def tok(i, _):
        at = pl.ds(pl.multiple_of(i * 32, 32), 32)
        ox[h, at, :] = d_one[h, at, :] + (xd[z, at, :].astype(F32) + x5[at, :].astype(F32))
        ox[1 - h, at, :] = d_one[1 - h, at, :] + x4[at, :].astype(F32)
        return 0

    lax.fori_loop(0, span // 32, tok, 0)
    for k in range(1, 8):
        src = (t + 8 - k) % 8
        got(qr.at[src], s_qe.at[0, k - 1], r_qe.at[0, k - 1], (d, src))
        got(vr.at[src], s_qe.at[1, k - 1], r_qe.at[1, k - 1], (d, src))
    for g in range(4):
        oq[g] = qr[g].astype(F32) + qr[4 + g].astype(F32)
    total = vr[0]
    for k in range(1, 8):
        total = total + vr[k]
    ov[...] = total
    for cp in sends:
        cp.wait_send()
    for n_ in range(2):
        @pl.when(jnp.logical_not(inner))
        def _(n_=n_):
            for a in range(5):
                to_inner(a, n_).wait_send()

        @pl.when(inner)
        def _(n_=n_):
            for a in range(5):
                to_far(a, n_).wait_send()


NEAR = (0, 1, 7, 2, 6, 3, 5, 4)


def back(dat, di, do_, db, ds_, qkv, ids, o32, lse, wt, xs, d_one):
    arrs = [di, do_, db, ds_]
    tails = [a.shape[4:] for a in arrs]
    per, width = wt.shape[2:]
    n = qkv.shape[2]
    tok = xs.shape[1:]
    qt = di.shape[4:6] + (3 * per,)
    vt = (8, 128)
    scratch = []
    for lead in ((2, 2, 4), (2, 2, 4), (4, 2), (4,), (2,), (), ()):
        for a, tail in zip(arrs, tails):
            scratch.append(pltpu.VMEM(lead + tail, a.dtype))
    grid = (2, 2, 4, 2)
    scratch += [
        pltpu.VMEM(dat.shape, BF),
        pltpu.VMEM((NH, n, 80), BF), pltpu.VMEM((NH, 80, n), BF), pltpu.VMEM((NH, n, 64), BF),
        pltpu.VMEM((NH, n, 128), F32), pltpu.VMEM((3, per, n), BF),
        pltpu.VMEM(xs.shape, BF), pltpu.VMEM(xs.shape, BF), pltpu.VMEM((3 * per, width), F32),
        pltpu.VMEM(grid + qt, BF), pltpu.VMEM(grid + vt, F32),
        pltpu.VMEM((4,) + tok, BF), pltpu.VMEM((2,) + tok, BF), pltpu.VMEM(tok, BF), pltpu.VMEM(tok, BF),
        pltpu.VMEM((2, 4, 2) + qt, BF), pltpu.VMEM((2, 4, 2) + qt, BF), pltpu.VMEM((4, 2) + qt, BF),
        pltpu.VMEM((8,) + qt, BF),
        pltpu.VMEM((2, 4, 2) + vt, F32), pltpu.VMEM((2, 4, 2) + vt, F32), pltpu.VMEM((4, 2) + vt, F32),
        pltpu.VMEM((8,) + vt, F32),
        dma(10), dma(7), dma(7), dma(9, 4), dma(9, 4), dma(4, 4), dma(4, 4), dma(4, 4), dma(4, 4),
        dma(5, 2), dma(5, 2), dma(5, 2), dma(5), dma(5), dma(5),
        dma(2), dma(2), dma(2), dma(2), dma(2, 7), dma(2, 7),
    ]
    return pl.pallas_call(
        back_kernel,
        out_shape=[jax.ShapeDtypeStruct((2,) + tok, F32)]
        + [jax.ShapeDtypeStruct(tail, F32) for tail in tails]
        + [jax.ShapeDtypeStruct((4,) + qt, F32), jax.ShapeDtypeStruct(vt, F32)],
        in_specs=[any_spec()] * 5 + [vmem_spec()] * 5 + [any_spec(), vmem_spec()],
        out_specs=[vmem_spec()] * 7,
        scratch_shapes=scratch,
        compiler_params=pltpu.CompilerParams(
            collective_id=4, has_side_effects=True, vmem_limit_bytes=VMEM_LIMIT),
        name="back",
    )(dat, di, do_, db, ds_, qkv, ids, o32, lse, wt, xs, d_one)


def erf_parts(u):
    phi_c = 0.5 * (1.0 + lax.erf(u * 0.7071067811865476))
    return phi_c, phi_c + u * jnp.exp(-0.5 * u * u) * 0.3989422804014327


def norm_forward(r):
    center = r - jnp.mean(r, axis=-1, keepdims=True)
    inv = lax.rsqrt(jnp.mean(center * center, axis=-1, keepdims=True) + layer_eps)
    return center * inv, inv


def norm_backward(n, inv, gain, dy):
    gd = gain * dy
    return (gd - jnp.mean(gd, axis=-1, keepdims=True) - n * jnp.mean(gd * n, axis=-1, keepdims=True)) * inv


def mid_kernel(x, att, wo, wi, wb, fv, bi, cot,
               out, d_one, dat, g_in, g_out, g_back, g_small,
               vo, vi, vb, att_t, acc, n1, inv1, low, low_t, slope, act, act_t, d_pre, d_two, d_br, d_attn,
               yi, yo, yb, yx, yd, ys, part, sums, sum_in, sem_w, sem_o):
    tokens, width = x.shape
    span = tokens // 2
    ff = vi.shape[1]
    loads = [pltpu.make_async_copy(a, b, sem_w.at[k]) for k, (a, b) in enumerate(((wo, vo), (wi, vi), (wb, vb)))]
    for cp in loads:
        cp.start()
    outs = []

    def put(src, to):
        cp = pltpu.make_async_copy(src, to, sem_o.at[len(outs)])
        cp.start()
        outs.append(cp)

    def loop(count, size, fn):
        def one(j, _):
            fn(pl.ds(pl.multiple_of(j * size, size), size))
            return 0

        lax.fori_loop(0, count, one, 0)

    halves = (slice(0, span), slice(span, tokens))
    rb = tokens // 4
    nt = (((1,), (1,)), ((), ()))
    part[...] = jnp.zeros_like(part)

    def count_in(k, v):
        part[k] += jnp.sum(v.reshape(v.shape[0] // 8, 8, width), axis=0)

    for s in range(2):
        att_t[halves[s]] = att[s].astype(F32).T.astype(BF)
    loads[0].wait()
    for s in range(2):
        acc[halves[s]] = jnp.dot(att_t[halves[s]], vo[...], preferred_element_type=F32)

    def norm_one(r):
        n, inv = norm_forward(x[r].astype(F32) + acc[r] + fv[2:3])
        n1[r] = n
        inv1[r] = inv
        low[r] = (n * fv[3:4] + fv[4:5]).astype(BF)

    loop(4, rb, norm_one)
    loads[1].wait()

    def widen(f):
        pre = [jnp.dot(low[r], vi[:, f], preferred_element_type=F32) + bi[:, f] for r in halves]
        for r, u in zip(halves, pre):
            phi_c, sl = erf_parts(u)
            slope[r, f] = sl
            a = u * phi_c
            act[r, f] = a.astype(BF)
            act_t[f, r] = a.T.astype(BF)

    loop(ff // 256, 256, widen)
    loads[2].wait()

    def narrow(f):
        for r in halves:
            acc[r, f] = jnp.dot(act[r], vb[:, f], preferred_element_type=F32)

    loop(width // 256, 256, narrow)

    def norm_two(r):
        normed = n1[r] * fv[3:4] + fv[4:5]
        n2, inv2 = norm_forward(normed + acc[r] + fv[5:6])
        yx[r] = (n2 * fv[6:7] + fv[7:8]).astype(BF)
        dy = cot[r].astype(F32)
        d2 = norm_backward(n2, inv2, fv[6:7], dy)
        d_two[r] = d2
        d2 = d2.astype(BF)
        d_br[r] = d2
        count_in(3, d2.astype(F32))
        count_in(4, dy * n2)
        count_in(5, dy)

    loop(4, rb, norm_two)
    put(yx, out)

    def back_widen(f):
        da = [lax.dot_general(d_br[r], vb[f, :], nt, preferred_element_type=F32) for r in halves]
        total = None
        for r, v in zip(halves, da):
            dp = (v * slope[r, f]).astype(BF)
            d_pre[r, f] = dp
            col = jnp.sum(dp.astype(F32), axis=0, keepdims=True)
            total = col if total is None else total + col
        sum_in[:, f] = total

    loop(ff // 256, 256, back_widen)

    def back_narrow(k):
        for r in halves:
            acc[r, k] = lax.dot_general(d_pre[r], vi[k, :], nt, preferred_element_type=F32)

    loop(width // 256, 256, back_narrow)

    def back_one(r):
        dn = d_two[r] + acc[r]
        n = n1[r]
        d1 = norm_backward(n, inv1[r], fv[3:4], dn)
        d_one[r] = d1
        d1 = d1.astype(BF)
        d_attn[r] = d1
        count_in(0, d1.astype(F32))
        count_in(1, dn * n)
        count_in(2, dn)

    loop(4, rb, back_one)
    for s in range(2):
        yd[s] = lax.dot_general(vo[...], d_attn[halves[s]], nt, preferred_element_type=F32).astype(BF)
    put(yd, dat)

    def grad_back(f):
        yb[f, :] = jnp.dot(act_t[f, :], d_br[...], preferred_element_type=F32).astype(BF)

    loop(ff // 256, 256, grad_back)
    put(yb, g_back)
    for k in range(3):
        low_t[k * 256:(k + 1) * 256] = low[:, k * 256:(k + 1) * 256].astype(F32).T.astype(BF)
    for k in range(3):
        rows = slice(k * 256, (k + 1) * 256)

        def grad_in(f, rows=rows):
            yi[rows, f] = jnp.dot(low_t[rows], d_pre[:, f], preferred_element_type=F32).astype(BF)

        loop(ff // 768, 768, grad_in)
        put(yi.at[rows], g_in.at[rows])

    def grad_out(k):
        yo[k] = (jnp.dot(att[0, k], d_attn[halves[0]], preferred_element_type=F32)
                 + jnp.dot(att[1, k], d_attn[halves[1]], preferred_element_type=F32)).astype(BF)

    loop(3, 256, grad_out)
    put(yo, g_out)
    ys[...] = jnp.zeros_like(ys)
    for k in range(6):
        sums[k:k + 1] = jnp.sum(part[k], axis=0, keepdims=True)
    for r in range(32):
        at = (r // 16, (r // 8) % 2, (r // 2) % 4, r % 2)
        ys[at + (slice(0, 6), slice(0, 24))] = sums[0:6, 24 * r:24 * r + 24]
        ys[at + (slice(6, 7), slice(0, 96))] = sum_in[:, 96 * r:96 * r + 96]
    put(ys, g_small)
    for cp in outs:
        cp.wait()


def mid(x, att, wo, wi, wb, fv, bi, cot):
    tokens, width = x.shape
    ff = wi.shape[1]
    tok = lambda dt: pltpu.VMEM((tokens, width), dt)
    wide = lambda dt: pltpu.VMEM((tokens, ff), dt)
    owner = (2, 2, 4, 2, 8, 128)
    shape = jax.ShapeDtypeStruct
    return pl.pallas_call(
        mid_kernel,
        out_shape=[
            shape((tokens, width), BF), shape((tokens, width), F32), shape(att.shape, BF), shape(wi.shape, BF),
            shape(wo.shape, BF), shape(wb.shape, BF), shape(owner, F32),
        ],
        in_specs=[vmem_spec()] * 2 + [any_spec()] * 3 + [vmem_spec()] * 3,
        out_specs=[any_spec(), vmem_spec()] + [any_spec()] * 5,
        scratch_shapes=[
            pltpu.VMEM(wo.shape, BF), pltpu.VMEM(wi.shape, BF), pltpu.VMEM(wb.shape, BF),
            tok(BF), tok(F32), tok(F32), pltpu.VMEM((tokens, 1), F32), tok(BF), pltpu.VMEM((width, tokens), BF),
            wide(F32), wide(BF), pltpu.VMEM((ff, tokens), BF), wide(BF), tok(F32), tok(BF), tok(BF),
            pltpu.VMEM(wi.shape, BF), pltpu.VMEM(wo.shape, BF), pltpu.VMEM(wb.shape, BF),
            tok(BF), pltpu.VMEM(att.shape, BF), pltpu.VMEM(owner, F32),
            pltpu.VMEM((6, 8, width), F32), pltpu.VMEM((8, width), F32), pltpu.VMEM((1, ff), F32),
            dma(3), dma(8),
        ],
        compiler_params=pltpu.CompilerParams(vmem_limit_bytes=VMEM_LIMIT),
        name="mid",
    )(x, att, wo, wi, wb, fv, bi, cot)


def on_device_fast(
    inputs, segments, w_qkv, b_query, b_value, w_out, b_attn, gain_one, shift_one,
    w_in, b_in, w_back, b_back, gain_two, shift_two, cotangent,
):
    nseq, span, width = inputs.shape
    tokens = nseq * span
    ff = w_in.shape[1]
    depth = w_in.shape[0]
    d, t, z, c, _, _ = place()
    per = width // 4
    vecs = (b_query, b_value, b_attn, gain_one, shift_one, b_back, gain_two, shift_two)
    ffd = b_in.shape[0]
    nv = len(vecs)
    small = jnp.pad(jnp.stack(vecs).astype(F32), ((0, 8), (0, 128 - depth)))
    small = lax.dynamic_update_slice(small, b_in.astype(F32)[None], (nv, 0))
    idb = jnp.broadcast_to(segments.astype(F32)[:, None], (nseq, 8, span))
    xs, ids, gi, go, gb, fv, bi, att, qkv, o32, lse, wt = front(
        inputs, idb, w_in.reshape(depth // 8, 8, ff), w_out.reshape(depth // 8, 8, width),
        w_back.reshape(ffd // 8, 8, width), small, w_qkv.reshape(depth // 8, 8, 3 * width))
    output, d_one, d_att, grad_w_in, grad_w_out, grad_w_back, g_small = mid(
        inputs.reshape(tokens, width), att.reshape(nseq, width, span), go.reshape(width, width),
        gi.reshape(width, ff), gb.reshape(ff, width), fv, bi, cotangent.reshape(tokens, width))
    output = output.reshape(nseq, span, width)
    owner = (2, 2, 4, 2)
    input_grad, oi, oo, ob, os_, oq, ov = back(
        d_att.reshape(8, per, span),
        grad_w_in.reshape(owner + (depth // 8, 8, ff)),
        grad_w_out.reshape(owner + (depth // 8, 8, width)),
        grad_w_back.reshape(owner + (ffd // 8, 8, width)),
        g_small, qkv, ids, o32, lse, wt, xs, d_one.reshape(nseq, span, width),
    )
    g_qkv = oq.reshape(4, depth, 3, per).transpose(1, 2, 0, 3).reshape(depth, 3 * width)
    vec = lambda k: os_[k, :depth]
    return (
        output, input_grad, g_qkv, ov[0, :depth], ov[1, :depth], oo.reshape(depth, width), vec(0), vec(1), vec(2),
        oi.reshape(depth, ff), os_[6, :ffd], ob.reshape(ffd, width),
        vec(3), vec(4), vec(5),
    )


negative_fill = -1e30


def layer_norm(resid, gain, shift):
    center = resid - jnp.mean(resid, axis=-1, keepdims=True)
    spread = jnp.mean(center * center, axis=-1, keepdims=True)
    return center * lax.rsqrt(spread + layer_eps) * gain + shift


def gelu_exact(values):
    return jax.nn.gelu(values, approximate=False)


def attend_forward(entries):
    query_rows, key_rows, value_rows, query_ids, key_ids = entries
    scores = jnp.einsum(
        "qhd,khd->hqk", query_rows, key_rows, preferred_element_type=jnp.float32
    ) * HEAD_DIM ** (-0.5)
    allowed = (query_ids[:, None] == key_ids[None, :])[None]
    scores = jnp.where(allowed, scores, negative_fill)
    peak = jnp.max(scores, axis=-1, keepdims=True)
    raised = jnp.exp(scores - peak)
    total = jnp.sum(raised, axis=-1, keepdims=True)
    probs_low = (raised / total).astype(jnp.bfloat16)
    context = jnp.einsum("hqk,khd->qhd", probs_low, value_rows, preferred_element_type=jnp.float32)
    return (context, (peak + jnp.log(total))[..., 0])


def score_terms(query_rows, key_rows, value_rows, grad_context, log_total, query_ids, key_ids):
    scale = HEAD_DIM ** (-0.5)
    scores = (
        jnp.einsum("qhd,khd->hqk", query_rows, key_rows, preferred_element_type=jnp.float32) * scale
    )
    allowed = (query_ids[:, None] == key_ids[None, :])[None]
    probs = jnp.where(allowed, jnp.exp(scores - log_total[..., None]), 0.0)
    d_probs = jnp.einsum(
        "qhd,khd->hqk", grad_context, value_rows, preferred_element_type=jnp.float32
    )
    return (probs, d_probs)


def attend_backward(entries):
    query_rows, key_rows, value_rows, grad_context, log_total, query_ids, key_ids = entries
    scale = HEAD_DIM ** (-0.5)
    probs, d_probs = score_terms(
        query_rows, key_rows, value_rows, grad_context, log_total, query_ids, key_ids
    )
    inner = jnp.sum(probs * d_probs, axis=-1, keepdims=True)
    d_scores = (probs * (d_probs - inner)).astype(jnp.bfloat16)
    d_queries = (
        jnp.einsum("hqk,khd->qhd", d_scores, key_rows, preferred_element_type=jnp.float32) * scale
    )
    d_keys = (
        jnp.einsum("hqk,qhd->khd", d_scores, query_rows, preferred_element_type=jnp.float32) * scale
    )
    d_values = jnp.einsum(
        "hqk,qhd->khd", probs.astype(jnp.bfloat16), grad_context, preferred_element_type=jnp.float32
    )
    length = key_rows.shape[0]
    return (
        d_queries,
        d_keys.reshape(length, HEADS * HEAD_DIM),
        d_values.reshape(length, HEADS * HEAD_DIM),
    )


def on_device_general(
    inputs,
    segments,
    w_qkv,
    b_query,
    b_value,
    w_out,
    b_attn,
    gain_one,
    shift_one,
    w_in,
    b_in,
    w_back,
    b_back,
    gain_two,
    shift_two,
    cotangent,
):
    seq_count, group_len, model_width = inputs.shape
    tok_count = seq_count * group_len
    gathered = (
        lax.all_gather(w_qkv, ("dp", "ctx"), axis=0, tiled=True),
        lax.all_gather(b_query, ("dp", "ctx"), axis=0, tiled=True),
        lax.all_gather(b_value, ("dp", "ctx"), axis=0, tiled=True),
        lax.all_gather(w_out, ("dp", "ctx"), axis=0, tiled=True),
        lax.all_gather(b_attn, ("dp", "ctx"), axis=0, tiled=True),
        lax.all_gather(gain_one, ("dp", "ctx"), axis=0, tiled=True),
        lax.all_gather(shift_one, ("dp", "ctx"), axis=0, tiled=True),
        lax.all_gather(w_in, ("dp", "ctx"), axis=0, tiled=True),
        lax.all_gather(b_in, ("dp", "ctx"), axis=0, tiled=True),
        lax.all_gather(w_back, ("dp", "ctx"), axis=0, tiled=True),
        lax.all_gather(b_back, ("dp", "ctx"), axis=0, tiled=True),
        lax.all_gather(gain_two, ("dp", "ctx"), axis=0, tiled=True),
        lax.all_gather(shift_two, ("dp", "ctx"), axis=0, tiled=True),
    )
    (
        wide_qkv,
        full_b_query,
        full_b_value,
        wide_out,
        full_b_attn,
        full_gain_one,
        full_shift_one,
        wide_in,
        full_b_in,
        wide_back,
        full_b_back,
        full_gain_two,
        full_shift_two,
    ) = gathered
    tokens = inputs.reshape(tok_count, model_width)
    projected = jnp.dot(tokens, wide_qkv, preferred_element_type=jnp.float32)
    query_low = (projected[:, :model_width] + full_b_query.astype(jnp.float32)).astype(jnp.bfloat16)
    key_low = projected[:, model_width : 2 * model_width].astype(jnp.bfloat16)
    value_low = (projected[:, 2 * model_width :] + full_b_value.astype(jnp.float32)).astype(
        jnp.bfloat16
    )
    key_ids = lax.all_gather(segments, "ctx", axis=1, tiled=True)
    key_local = key_low.reshape(seq_count, group_len, model_width)
    value_local = value_low.reshape(seq_count, group_len, model_width)
    key_whole, value_whole = (
        lax.all_gather(key_local, "ctx", axis=1, tiled=True),
        lax.all_gather(value_local, "ctx", axis=1, tiled=True),
    )
    seq_len = key_whole.shape[1]
    query_heads = query_low.reshape(seq_count, group_len, HEADS, HEAD_DIM)
    context, log_total = lax.map(
        attend_forward,
        (
            query_heads,
            key_whole.reshape(seq_count, seq_len, HEADS, HEAD_DIM),
            value_whole.reshape(seq_count, seq_len, HEADS, HEAD_DIM),
            segments,
            key_ids,
        ),
    )
    attended = context.reshape(tok_count, model_width).astype(jnp.bfloat16)
    attn_out = jnp.dot(attended, wide_out, preferred_element_type=jnp.float32) + full_b_attn.astype(
        jnp.float32
    )
    resid_one = tokens.astype(jnp.float32) + attn_out
    normed, norm_one_back = jax.vjp(
        layer_norm, resid_one, full_gain_one.astype(jnp.float32), full_shift_one.astype(jnp.float32)
    )
    normed_low = normed.astype(jnp.bfloat16)
    pre_act = jnp.dot(normed_low, wide_in, preferred_element_type=jnp.float32) + full_b_in.astype(
        jnp.float32
    )
    activ_f, gelu_back = jax.vjp(gelu_exact, pre_act)
    activ = activ_f.astype(jnp.bfloat16)
    branch = jnp.dot(activ, wide_back, preferred_element_type=jnp.float32) + full_b_back.astype(
        jnp.float32
    )
    resid_two = normed + branch
    final_norm, norm_two_back = jax.vjp(
        layer_norm, resid_two, full_gain_two.astype(jnp.float32), full_shift_two.astype(jnp.float32)
    )
    output = final_norm.astype(jnp.bfloat16).reshape(seq_count, group_len, model_width)
    back_qkv, back_out, back_in, back_back = (
        lax.all_gather(w_qkv, ("dp", "ctx"), axis=0, tiled=True),
        lax.all_gather(w_out, ("dp", "ctx"), axis=0, tiled=True),
        lax.all_gather(w_in, ("dp", "ctx"), axis=0, tiled=True),
        lax.all_gather(w_back, ("dp", "ctx"), axis=0, tiled=True),
    )
    d_final = cotangent.reshape(tok_count, model_width).astype(jnp.float32)
    d_two, grad_gain_two, grad_shift_two = norm_two_back(d_final)
    d_branch = d_two.astype(jnp.bfloat16)
    grad_b_back = jnp.sum(d_branch.astype(jnp.float32), axis=0)
    grad_w_back = jnp.einsum("tf,td->fd", activ, d_branch, preferred_element_type=jnp.float32)
    d_activ = jnp.einsum("td,fd->tf", d_branch, back_back, preferred_element_type=jnp.float32)
    d_pre = gelu_back(d_activ)[0].astype(jnp.bfloat16)
    grad_b_in = jnp.sum(d_pre.astype(jnp.float32), axis=0)
    grad_w_in = jnp.einsum("td,tf->df", normed_low, d_pre, preferred_element_type=jnp.float32)
    d_normed = d_two + jnp.einsum("tf,df->td", d_pre, back_in, preferred_element_type=jnp.float32)
    d_one, grad_gain_one, grad_shift_one = norm_one_back(d_normed)
    d_attn = d_one.astype(jnp.bfloat16)
    grad_b_attn = jnp.sum(d_attn.astype(jnp.float32), axis=0)
    grad_w_out = jnp.einsum("ti,td->id", attended, d_attn, preferred_element_type=jnp.float32)
    d_attended = jnp.einsum(
        "td,id->ti", d_attn, back_out, preferred_element_type=jnp.float32
    ).astype(jnp.bfloat16)
    key_back, value_back = (
        lax.all_gather(key_local, "ctx", axis=1, tiled=True),
        lax.all_gather(value_local, "ctx", axis=1, tiled=True),
    )
    grad_heads = d_attended.reshape(seq_count, group_len, HEADS, HEAD_DIM)
    d_query_part, d_key_part, d_value_part = lax.map(
        attend_backward,
        (
            query_heads,
            key_back.reshape(seq_count, seq_len, HEADS, HEAD_DIM),
            value_back.reshape(seq_count, seq_len, HEADS, HEAD_DIM),
            grad_heads,
            log_total,
            segments,
            key_ids,
        ),
    )
    d_key_sum, d_value_sum = (
        lax.psum_scatter(
            d_key_part.astype(jnp.bfloat16), "ctx", scatter_dimension=1, tiled=True
        ).astype(jnp.float32),
        lax.psum_scatter(
            d_value_part.astype(jnp.bfloat16), "ctx", scatter_dimension=1, tiled=True
        ).astype(jnp.float32),
    )
    d_queries = d_query_part.reshape(tok_count, model_width).astype(jnp.bfloat16)
    d_keys = d_key_sum.reshape(tok_count, model_width).astype(jnp.bfloat16)
    d_values = d_value_sum.reshape(tok_count, model_width).astype(jnp.bfloat16)
    d_proj = jnp.concatenate([d_queries, d_keys, d_values], axis=1)
    grad_w_qkv = jnp.einsum("td,te->de", tokens, d_proj, preferred_element_type=jnp.float32)
    grad_b_query = jnp.sum(d_queries.astype(jnp.float32), axis=0)
    grad_b_value = jnp.sum(d_values.astype(jnp.float32), axis=0)
    input_grad = d_one + jnp.einsum(
        "te,de->td", d_proj, back_qkv, preferred_element_type=jnp.float32
    )
    summed = (
        lax.psum_scatter(grad_w_qkv, ("dp", "ctx"), scatter_dimension=0, tiled=True),
        lax.psum_scatter(grad_b_query, ("dp", "ctx"), scatter_dimension=0, tiled=True),
        lax.psum_scatter(grad_b_value, ("dp", "ctx"), scatter_dimension=0, tiled=True),
        lax.psum_scatter(grad_w_out, ("dp", "ctx"), scatter_dimension=0, tiled=True),
        lax.psum_scatter(grad_b_attn, ("dp", "ctx"), scatter_dimension=0, tiled=True),
        lax.psum_scatter(grad_gain_one, ("dp", "ctx"), scatter_dimension=0, tiled=True),
        lax.psum_scatter(grad_shift_one, ("dp", "ctx"), scatter_dimension=0, tiled=True),
        lax.psum_scatter(grad_w_in, ("dp", "ctx"), scatter_dimension=0, tiled=True),
        lax.psum_scatter(grad_b_in, ("dp", "ctx"), scatter_dimension=0, tiled=True),
        lax.psum_scatter(grad_w_back, ("dp", "ctx"), scatter_dimension=0, tiled=True),
        lax.psum_scatter(grad_b_back, ("dp", "ctx"), scatter_dimension=0, tiled=True),
        lax.psum_scatter(grad_gain_two, ("dp", "ctx"), scatter_dimension=0, tiled=True),
        lax.psum_scatter(grad_shift_two, ("dp", "ctx"), scatter_dimension=0, tiled=True),
    )
    return (
        output,
        input_grad.reshape(seq_count, group_len, model_width),
        summed[0],
        summed[1],
        summed[2],
        summed[3],
        summed[4],
        summed[5],
        summed[6],
        summed[7],
        summed[8],
        summed[9],
        summed[10],
        summed[11],
        summed[12],
    )


def solution(mesh):
    placed = (
        P("dp", "ctx", None),
        P("dp", "ctx"),
        P(("dp", "ctx"), None),
        P(("dp", "ctx")),
        P(("dp", "ctx")),
        P(("dp", "ctx"), None),
        P(("dp", "ctx")),
        P(("dp", "ctx")),
        P(("dp", "ctx")),
        P(("dp", "ctx"), None),
        P(("dp", "ctx")),
        P(("dp", "ctx"), None),
        P(("dp", "ctx")),
        P(("dp", "ctx")),
        P(("dp", "ctx")),
        P("dp", "ctx", None),
    )
    fits = mesh.shape["dp"] == 4 and mesh.shape["ctx"] == 8
    return jax.shard_map(
        on_device_fast if fits else on_device_general,
        mesh=mesh,
        in_specs=placed,
        out_specs=(
            P("dp", "ctx", None),
            P("dp", "ctx", None),
            P(("dp", "ctx"), None),
            P(("dp", "ctx")),
            P(("dp", "ctx")),
            P(("dp", "ctx"), None),
            P(("dp", "ctx")),
            P(("dp", "ctx")),
            P(("dp", "ctx")),
            P(("dp", "ctx"), None),
            P(("dp", "ctx")),
            P(("dp", "ctx"), None),
            P(("dp", "ctx")),
            P(("dp", "ctx")),
            P(("dp", "ctx")),
        ),
        check_vma=False,
    )
```

profile of v0, /device:TPU:28, one launch (start us, length us, event | category | flops | bytes accessed | tf_op | source)
XLA Modules:
  0.0 246.2 jit_solution(16408860607412807976)
XLA Ops:
  0.6 0.7 bitcast_convert_fusion
  1.3 0.7 convert_element_type.4
  2.0 0.8 stack.35
  2.8 0.6 pad_convert_fusion
  3.4 1.3 dynamic_update_slice.3.sm
  4.7 0.6 broadcast_in_dim.12.idb
  5.3 93.6 %front.1 = (bf16[8,256,768]{2,1,0:T(8,128)(2,1)}, f32[8,8,256]{2,1,0:T(8,128)}, bf16[4,4,2,3,8,3072]{5,4,3,2,1,0:T(8,128)(2,1)}, bf16[4,4,2,3,8,768]{5,4,3,2,1,0...) custom-call(bf16[2,256,768]{2,1,0:T(8,128)(2,1)} %x.3, ...), custom_call_target="tpu_custom_call" | custom-call | tf_op jit(solution)/shard_map/front/pallas_call | solution.py:383
  98.9 39.6 %mid.1 = (bf16[512,768]{1,0:T(8,128)(2,1)}, f32[512,768]{1,0:T(8,128)}, bf16[2,768,256]{2,1,0:T(8,128)(2,1)}, bf16[768,3072]{1,0:T(8,128)(2,1)}, bf16[768,768]{1...) custom-call(bf16[512,768]{1,0:T(8,128)(2,1)} %bitcast.55, bf16[2,768,256]{2,1,0:T(8,128)(2,1)} %bitcast.62, ...), custom_call_target="tpu_custom_call" | custom-call | tf_op jit(solution)/shard_map/mid/pallas_call | solution.py:949
  138.5 99.5 %back.1 = (f32[2,256,768]{2,1,0:T(8,128)}, f32[3,8,3072]{2,1,0:T(8,128)}, f32[3,8,768]{2,1,0:T(8,128)}, f32[12,8,768]{2,1,0:T(8,128)}, f32[8,128]{1,0:T(8,128)},...) custom-call(bf16[8,192,256]{2,1,0:T(8,128)(2,1)} %bitcast.60, bf16[2,2,4,2,3,8,3072]{6,5,4,3,2,1,0:T(8,128)(2,1)} %bitcast.53, ...), custom_call_target="tpu_custom_call" | custom-call | tf_op jit(solution)/shard_map/back/pallas_call | solution.py:763
  238.0 0.0 copy-start
  238.0 1.3 slice_bitcast_fusion.3
  239.4 1.4 slice_bitcast_fusion
  240.8 1.1 reshape.110
  241.9 0.2 copy.32
  242.1 0.0 copy-start.3
  242.1 0.9 reshape.111
  243.0 0.0 copy-done
  243.0 0.0 copy-start.2
  243.0 0.0 copy-start.1
  243.0 1.1 copy.38
  244.2 0.0 copy-done.3
  244.2 0.6 copy.39
  244.8 0.0 copy-done.2
  244.8 0.7 copy.40
  245.5 0.0 copy-done.1
  245.5 0.7 copy.41
Async XLA Ops:
  238.0 5.0 %copy-start = (f32[2,256,768]{2,1,0:T(8,128)S(1)}, f32[2,256,768]{2,1,0:T(8,128)}, u32[]{:S(2)}) copy-start(f32[2,256,768]{2,1,0:T(8,128)} %get-tuple-element.93) | copy-start | bytes 4718596
  242.1 2.0 copy-start.3
  243.0 1.8 copy-start.2
  243.0 2.5 %copy-start.1 = (f32[12,8,768]{2,1,0:T(8,128)S(1)}, f32[12,8,768]{2,1,0:T(8,128)}, u32[]{:S(2)}) copy-start(f32[12,8,768]{2,1,0:T(8,128)} %get-tuple-element.66) | copy-start | bytes 884740
where the time goes:
time: 250 us; the launch traced here: 246 us
  Pallas kernels  233 us (93%)
  local copies, waits for them, and re-layouts  10.9 us (4%)
    pallas_call x1, Pallas kernels, back(): pl.pallas_call(back_kernel, out_shape=[jax.ShapeDtypeStruct((2,) + tok, F...  99.5 us
    pallas_call x1, Pallas kernels, front(): pl.pallas_call(front_kernel, out_shape=[jax.ShapeDtypeStruct((8, span, wi...  93.6 us
    pallas_call x1, Pallas kernels, mid(): pl.pallas_call(mid_kernel, out_shape=[shape((tokens, width), BF), shape((...  39.6 us

commit v1 on v0

--- a/solution.py
+++ b/solution.py
@@ -61,9 +61,9 @@
     return (i // 4) * (i % 4), 8 - (1 - i // 4) * (3 - i % 4)
 
 
-def front_kernel(x, idb, wi, wo, wb, sm, wq,
+def front_kernel(x, seg, wi, wo, wb, vs, bv, wq,
                  xs, ids, gi, go, gb, fv, bi, att, qkv, o32, lse, wt,
-                 gs, gq, ka, va, qa, sb,
+                 idb, sm, gs, gq, ka, va, qa, sb,
                  loc, s_x, r_x, s_xf, s_xd, r_xd, s_z, r_z, s_up, s_dn, s_px, r_px, s_py, r_py, s_f, r_f,
                  s_c, r_c, s_e, r_e):
     d, t, z, c, dx, dy = place()
@@ -77,6 +77,11 @@
     me = lambda zz: (d, zz * 2 + c)
     core = (d, z * 2 + 1 - c)
     nx, ny = (dx, t), (dy, t)
+    for hh in range(2):
+        idb[hh] = jnp.broadcast_to(seg[hh:hh + 1].astype(F32), idb.shape[1:])
+    sm[...] = jnp.zeros_like(sm)
+    sm[0:8, 0:24] = vs[...].astype(F32)
+    sm[8:9, 0:96] = bv[...].astype(F32)
     greet([(d, (t + k) % 8) for k in range(1, 8)] + [nx, ny])
     sends = []
 
@@ -375,7 +380,7 @@
     return pltpu.SemaphoreType.DMA(shape)
 
 
-def front(x, idb, wi, wo, wb, sm, wq):
+def front(x, seg, wi, wo, wb, vs, bv, wq):
     span, width = x.shape[1:]
     n = 8 * span
     per = width // 4
@@ -393,10 +398,10 @@
             jax.ShapeDtypeStruct((NH, 8, span), F32),
             jax.ShapeDtypeStruct((3, 2, per, width), BF),
         ],
-        in_specs=[any_spec()] * 7,
+        in_specs=[any_spec(), vmem_spec()] + [any_spec()] * 3 + [vmem_spec()] * 2 + [any_spec()],
         out_specs=[vmem_spec()] * 2 + [any_spec()] * 3 + [vmem_spec()] * 7,
         scratch_shapes=[
-            pltpu.VMEM((4, 4, 2) + sm.shape, F32),
+            pltpu.VMEM((2, 8, span), F32), pltpu.VMEM((16, 128), F32), pltpu.VMEM((4, 4, 2, 16, 128), F32),
             pltpu.VMEM((3, 4, 4, 2) + wq.shape[:2] + (2 * per,), BF),
             pltpu.VMEM((NH, n, 80), BF), pltpu.VMEM((NH, 80, n), BF), pltpu.VMEM((NH, 80, n), BF),
             pltpu.VMEM((8, per, span), BF),
@@ -408,11 +413,11 @@
         compiler_params=pltpu.CompilerParams(
             collective_id=1, has_side_effects=True, vmem_limit_bytes=VMEM_LIMIT),
         name="front",
-    )(x, idb, wi, wo, wb, sm, wq)
+    )(x, seg, wi, wo, wb, vs, bv, wq)
 
 
 def back_kernel(dat, di, do_, db, ds_, qkv, ids, o32, lse, wt, xs, d_one,
-                ox, oi, oo, ob, os_, oq, ov, *rest):
+                ox, oi, oo, ob, os_, oq, *rest):
     rd, own, r1, r2, r3, r4, r5 = [rest[4 * i:4 * i + 4] for i in range(7)]
     (da, ka, qa, vk, dkv, pr, xv, dxp, dw, lq, lv,
      xd, x3, x4, x5, q0, q1, q2, qr, v0, v1, v2, vr,
@@ -431,7 +436,7 @@
     order = [far[0], far[1], zp, z]
     group = (z % 2) * 2 + c
     part = [di, do_, db, ds_]
-    outs = [oi, oo, ob, os_]
+    outs = [oi, oo, ob, os_.at[pl.ds(0, 8)]]
     by_x = [True, True, False, True]
     sends = []
     greet([(d, o) for o in line] + [nx, ny])
@@ -714,7 +719,7 @@
     total = vr[0]
     for k in range(1, 8):
         total = total + vr[k]
-    ov[...] = total
+    os_[8:16] = total
     for cp in sends:
         cp.wait_send()
     for n_ in range(2):
@@ -763,10 +768,10 @@
     return pl.pallas_call(
         back_kernel,
         out_shape=[jax.ShapeDtypeStruct((2,) + tok, F32)]
-        + [jax.ShapeDtypeStruct(tail, F32) for tail in tails]
-        + [jax.ShapeDtypeStruct((4,) + qt, F32), jax.ShapeDtypeStruct(vt, F32)],
+        + [jax.ShapeDtypeStruct(tail, F32) for tail in tails[:3] + [(16, 128)]]
+        + [jax.ShapeDtypeStruct((4,) + qt, F32)],
         in_specs=[any_spec()] * 5 + [vmem_spec()] * 5 + [any_spec(), vmem_spec()],
-        out_specs=[vmem_spec()] * 7,
+        out_specs=[vmem_spec()] * 6,
         scratch_shapes=scratch,
         compiler_params=pltpu.CompilerParams(
             collective_id=4, has_side_effects=True, vmem_limit_bytes=VMEM_LIMIT),
@@ -968,6 +973,34 @@
     )(x, att, wo, wi, wb, fv, bi, cot)
 
 
+def finish_kernel(ix, oi, oo, ob, oq, px, pi, po, pb, pq, wide, sem):
+    copies = [pltpu.make_async_copy(a, b, sem.at[k]) for k, (a, b) in enumerate(((ix, px), (oi, pi), (ob, pb), (oo, po)))]
+    for cp in copies:
+        cp.start()
+    per = oq.shape[3] // 3
+    for g in range(4):
+        v = oq[g].reshape(wide.shape[0], 3 * per)
+        for k in range(3):
+            wide[:, (k * 4 + g) * per:(k * 4 + g + 1) * per] = v[:, k * per:(k + 1) * per]
+    copies.append(pltpu.make_async_copy(wide, pq, sem.at[4]))
+    copies[4].start()
+    for cp in copies:
+        cp.wait()
+
+
+def finish(ix, oi, oo, ob, oq):
+    shape = jax.ShapeDtypeStruct
+    wide = (oq.shape[1] * oq.shape[2], oq.shape[3] * 4)
+    return pl.pallas_call(
+        finish_kernel,
+        out_shape=[shape(a.shape, F32) for a in (ix, oi, oo, ob)] + [shape(wide, F32)],
+        in_specs=[vmem_spec()] * 5,
+        out_specs=[any_spec()] * 5,
+        scratch_shapes=[pltpu.VMEM(wide, F32), dma(5)],
+        name="finish",
+    )(ix, oi, oo, ob, oq)
+
+
 def on_device_fast(
     inputs, segments, w_qkv, b_query, b_value, w_out, b_attn, gain_one, shift_one,
     w_in, b_in, w_back, b_back, gain_two, shift_two, cotangent,
@@ -980,29 +1013,26 @@
     per = width // 4
     vecs = (b_query, b_value, b_attn, gain_one, shift_one, b_back, gain_two, shift_two)
     ffd = b_in.shape[0]
-    nv = len(vecs)
-    small = jnp.pad(jnp.stack(vecs).astype(F32), ((0, 8), (0, 128 - depth)))
-    small = lax.dynamic_update_slice(small, b_in.astype(F32)[None], (nv, 0))
-    idb = jnp.broadcast_to(segments.astype(F32)[:, None], (nseq, 8, span))
     xs, ids, gi, go, gb, fv, bi, att, qkv, o32, lse, wt = front(
-        inputs, idb, w_in.reshape(depth // 8, 8, ff), w_out.reshape(depth // 8, 8, width),
-        w_back.reshape(ffd // 8, 8, width), small, w_qkv.reshape(depth // 8, 8, 3 * width))
+        inputs, segments, w_in.reshape(depth // 8, 8, ff), w_out.reshape(depth // 8, 8, width),
+        w_back.reshape(ffd // 8, 8, width),
+        jnp.stack(vecs), b_in.reshape(1, ffd), w_qkv.reshape(depth // 8, 8, 3 * width))
     output, d_one, d_att, grad_w_in, grad_w_out, grad_w_back, g_small = mid(
         inputs.reshape(tokens, width), att.reshape(nseq, width, span), go.reshape(width, width),
         gi.reshape(width, ff), gb.reshape(ff, width), fv, bi, cotangent.reshape(tokens, width))
     output = output.reshape(nseq, span, width)
     owner = (2, 2, 4, 2)
-    input_grad, oi, oo, ob, os_, oq, ov = back(
+    input_grad, oi, oo, ob, os_, oq = back(
         d_att.reshape(8, per, span),
         grad_w_in.reshape(owner + (depth // 8, 8, ff)),
         grad_w_out.reshape(owner + (depth // 8, 8, width)),
         grad_w_back.reshape(owner + (ffd // 8, 8, width)),
         g_small, qkv, ids, o32, lse, wt, xs, d_one.reshape(nseq, span, width),
     )
-    g_qkv = oq.reshape(4, depth, 3, per).transpose(1, 2, 0, 3).reshape(depth, 3 * width)
+    input_grad, oi, oo, ob, g_qkv = finish(input_grad, oi, oo, ob, oq)
     vec = lambda k: os_[k, :depth]
     return (
-        output, input_grad, g_qkv, ov[0, :depth], ov[1, :depth], oo.reshape(depth, width), vec(0), vec(1), vec(2),
+        output, input_grad, g_qkv, vec(8), vec(9), oo.reshape(depth, width), vec(0), vec(1), vec(2),
         oi.reshape(depth, ff), os_[6, :ffd], ob.reshape(ffd, width),
         vec(3), vec(4), vec(5),
     )

time: 250 us -> 243 us (0.972)
  local copies, waits for them, and re-layouts: 10.9 us -> 2.43 us
  Pallas kernels: 233 us -> 236 us
    unnamed x12 -> x2, local copies, waits for them, and re-layouts: 3.22 us -> 0.01 us
    pallas_call x0 -> x1, Pallas kernels: none -> 3.09 us  [finish(): pl.pallas_call(finish_kernel, out_shape=[shape(a.shape, F32) for a in (ix...]
where the time goes in v1:
time: 243 us; the launch traced here: 239 us
  Pallas kernels  236 us (97%)
  local copies, waits for them, and re-layouts  2.43 us (1%)
    pallas_call x1, Pallas kernels, back(): pl.pallas_call(back_kernel, out_shape=[jax.ShapeDtypeStruct((2,) + tok, F...  99.3 us
    pallas_call x1, Pallas kernels, front(): pl.pallas_call(front_kernel, out_shape=[jax.ShapeDtypeStruct((8, span, wi...  94.3 us
    pallas_call x1, Pallas kernels, mid(): pl.pallas_call(mid_kernel, out_shape=[shape((tokens, width), BF), shape((...  39.7 us

profile of v1, /device:TPU:28, one launch (start us, length us, event | category | flops | bytes accessed | tf_op | source)
XLA Modules:
  0.0 239.5 jit_solution(13806576380021350628)
XLA Ops:
  0.6 1.4 stack.35.vs
  2.0 94.3 %front.1 = (bf16[8,256,768]{2,1,0:T(8,128)(2,1)}, f32[8,8,256]{2,1,0:T(8,128)}, bf16[4,4,2,3,8,3072]{5,4,3,2,1,0:T(8,128)(2,1)}, bf16[4,4,2,3,8,768]{5,4,3,2,1,0...) custom-call(bf16[2,256,768]{2,1,0:T(8,128)(2,1)} %x.1, ...), custom_call_target="tpu_custom_call" | custom-call | tf_op jit(solution)/shard_map/front/pallas_call | solution.py:388
  96.3 39.7 %mid.1 = (bf16[512,768]{1,0:T(8,128)(2,1)}, f32[512,768]{1,0:T(8,128)}, bf16[2,768,256]{2,1,0:T(8,128)(2,1)}, bf16[768,3072]{1,0:T(8,128)(2,1)}, bf16[768,768]{1...) custom-call(bf16[512,768]{1,0:T(8,128)(2,1)} %bitcast.50, bf16[2,768,256]{2,1,0:T(8,128)(2,1)} %bitcast.56, ...), custom_call_target="tpu_custom_call" | custom-call | tf_op jit(solution)/shard_map/mid/pallas_call | solution.py:954
  136.0 99.3 %back.1 = (f32[2,256,768]{2,1,0:T(8,128)}, f32[3,8,3072]{2,1,0:T(8,128)}, f32[3,8,768]{2,1,0:T(8,128)}, f32[12,8,768]{2,1,0:T(8,128)}, f32[16,128]{1,0:T(8,128)}, /*index=5*/f32[4,3,8,576]{3,2,1,0:T(8,128)}) custom-call(bf16[8,192,256]{2,1,0:T(8,128)(2,1)} %bitcast.54, bf16[2,2,4,2,3,8,3072]{6,5,4,3,2,1,0:T(8,128)(2,1)} %bitcast.48, ...), custom_call_target="tpu_custom_call" | custom-call | tf_op jit(solution)/shard_map/back/pallas_call | solution.py:768
  235.3 0.0 copy-start
  235.3 3.1 %finish.1 = (f32[2,256,768]{2,1,0:T(8,128)}, f32[3,8,3072]{2,1,0:T(8,128)}, f32[3,8,768]{2,1,0:T(8,128)}, f32[12,8,768]{2,1,0:T(8,128)}, f32[24,2304]{1,0:T(8,128)}) custom-call(f32[2,256,768]{2,1,0:T(8,128)} %get-tuple-element.64.ix, f32[3,8,3072]{2,1,0:T(8,128)} %get-tuple-element.65.oi, f32[3,8,768]{2,1,0:T(8,128)} %get-tuple-element.66.oo, ...), custom_call_target="tpu_custom_call" | custom-call | tf_op jit(solution)/shard_map/finish/pallas_call | solution.py:994
  238.4 0.0 copy-done
  238.4 0.5 slice_bitcast_fusion.3
  238.9 0.5 slice_bitcast_fusion
Async XLA Ops:
  235.3 3.1 %copy-start = (f32[16,128]{1,0:T(8,128)S(1)}, f32[16,128]{1,0:T(8,128)}, u32[]{:S(2)}) copy-start(f32[16,128]{1,0:T(8,128)} %get-tuple-element.71) | copy-start | bytes 24580

commit v2 on v1

--- a/solution.py
+++ b/solution.py
@@ -327,18 +327,18 @@
         plane(WIDE, others[k], False)
 
     order = ORDER_K
+    onward(0)
     attend(order[0])
-    onward(0)
     attend(order[1])
     for cp in locals_[7:]:
         cp.wait()
     across(WIDE, z)
+    onward(1)
     attend(order[2])
-    onward(1)
     attend(order[3])
     forward(WIDE, zp)
+    onward(2)
     attend(order[4])
-    onward(2)
     attend(order[5])
     forward(WIDE, z1)
     across(WIDE, zp)
@@ -632,12 +632,27 @@
         token_grad(j * 2 + 1 - c)
         return 0
 
+    per = pr.shape[1]
+    width = wt.shape[3]
+
+    def weight_grad(n_, q):
+        xall = xv[:, :, pl.ds(pl.multiple_of(q * (width // 2), 128), width // 2)].reshape(n, width // 2)
+        for s in range(3):
+            dw[s * per:(s + 1) * per] = jnp.dot(pr[s], xall, preferred_element_type=F32)
+        lq[q] = dw[...].T.reshape(lq.shape[1:]).astype(BF)
+        go_(remote(lq.at[q, 1 - x], q1.at[q], s_q1.at[n_], r_q1.at[n_], nx))
+
+    def summed(yy):
+        for zc in range(8):
+            at = (zc // 2, zc % 2)
+            q0[(yy,) + at] = q1[(yy,) + at] + lq[(yy, x) + at]
+
     lax.fori_loop(0, 4, token_pair, 0)
     for n_, zz in enumerate(order):
         go_(remote(dxp.at[zz * 2 + 1 - c], xd.at[zz], s_d.at[0, n_], r_d.at[0, n_], core))
     third(2)
     fourth(1, range(4))
-
+    weight_grad(0, 1 - y)
     def token_mine(j, _):
         token_grad(j * 2 + c)
         return 0
@@ -652,42 +667,27 @@
                 to_inner(4, n_).start()
         elif n_ == 2:
             go_(remote(xd.at[zz], x5, s_5.at[4], r_5.at[4], me(zz)))
-    per = pr.shape[1]
-    width = wt.shape[3]
-    xall = xv[...].reshape(n, width)
-    for s in range(3):
-        dw[s * per:(s + 1) * per] = jnp.dot(pr[s], xall, preferred_element_type=F32)
-    for q in range(2):
-        w = dw[:, q * (width // 2):(q + 1) * (width // 2)].T
-        lq[q] = w.reshape(lq.shape[1:]).astype(BF)
+    weight_grad(1, y)
     lv[...] = jnp.zeros_like(lv)
     for row, s in ((0, 0), (1, 2)):
         col = jnp.sum(pr[s].astype(F32), axis=1, keepdims=True)
         for r in range(8):
             piece = jnp.broadcast_to(col[24 * r:24 * r + 24], (24, 128)).T
             lv[group // 2, group % 2, r // 2, r % 2, row:row + 1, :24] = piece[0:1]
-    lq_x = lq
-    go_(remote(lq_x.at[:, 1 - x], q1, s_q1.at[0], r_q1.at[0], nx))
-    go_(remote(lv.at[:, 1 - x], v1, s_q1.at[1], r_q1.at[1], nx))
-    third(3)
-    fourth(0, (4,))
-    fourth(1, (4,))
-    got(q1, s_q1.at[0], r_q1.at[0], nx)
-    got(v1, s_q1.at[1], r_q1.at[1], nx)
+    go_(remote(lv.at[:, 1 - x], v1, s_q1.at[2], r_q1.at[2], nx))
+    got(q1.at[1 - y], s_q1.at[0], r_q1.at[0], nx)
+    summed(1 - y)
+    go_(remote(q0.at[1 - y], q2, s_q2.at[0], r_q2.at[0], ny))
+    got(v1, s_q1.at[2], r_q1.at[2], nx)
     for yy in range(2):
         for zc in range(8):
             at = (zc // 2, zc % 2)
-            q0[(yy,) + at] = q1[(yy,) + at] + lq[(yy, x) + at]
             v0[(yy,) + at] = v1[(yy,) + at] + lv[(yy, x) + at]
-    go_(remote(q0.at[1 - y], q2, s_q2.at[0], r_q2.at[0], ny))
     go_(remote(v0.at[1 - y], v2, s_q2.at[1], r_q2.at[1], ny))
-    src_in = 2 - h
-    for a in range(4):
-        got(r5[a], s_5.at[a], r_5.at[a], me(zp))
-        got(r4[a], s_4.at[a, 0], r_4.at[a], me(src_in))
-        acc = rd[a].at[y, x, z]
-        for i in range(acc.shape[0]):
-            outs[a][i] = acc[i].astype(F32) + r5[a][i].astype(F32) + r4[a][i].astype(F32)
+    third(3)
+    fourth(0, (4,))
+    got(q1.at[y], s_q1.at[1], r_q1.at[1], nx)
+    summed(y)
     got(q2, s_q2.at[0], r_q2.at[0], ny)
     got(v2, s_q2.at[1], r_q2.at[1], ny)
     for zc in range(8):
@@ -700,6 +700,14 @@
         go_(remote(v0.at[y, to // 2, to % 2], vr.at[t], s_qe.at[1, k - 1], r_qe.at[1, k - 1], (d, to)))
     qr[t] = q0[y, z, c]
     vr[t] = v0[y, z, c]
+    fourth(1, (4,))
+    src_in = 2 - h
+    for a in range(4):
+        got(r5[a], s_5.at[a], r_5.at[a], me(zp))
+        got(r4[a], s_4.at[a, 0], r_4.at[a], me(src_in))
+        acc = rd[a].at[y, x, z]
+        for i in range(acc.shape[0]):
+            outs[a][i] = acc[i].astype(F32) + r5[a][i].astype(F32) + r4[a][i].astype(F32)
     got(x5, s_5.at[4], r_5.at[4], me(zp))
     got(x4, s_4.at[4, 0], r_4.at[4], me(src_in))
 
@@ -754,7 +762,7 @@
         pltpu.VMEM(dat.shape, BF),
         pltpu.VMEM((NH, n, 80), BF), pltpu.VMEM((NH, 80, n), BF), pltpu.VMEM((NH, n, 64), BF),
         pltpu.VMEM((NH, n, 128), F32), pltpu.VMEM((3, per, n), BF),
-        pltpu.VMEM(xs.shape, BF), pltpu.VMEM(xs.shape, BF), pltpu.VMEM((3 * per, width), F32),
+        pltpu.VMEM(xs.shape, BF), pltpu.VMEM(xs.shape, BF), pltpu.VMEM((3 * per, width // 2), F32),
         pltpu.VMEM(grid + qt, BF), pltpu.VMEM(grid + vt, F32),
         pltpu.VMEM((4,) + tok, BF), pltpu.VMEM((2,) + tok, BF), pltpu.VMEM(tok, BF), pltpu.VMEM(tok, BF),
         pltpu.VMEM((2, 4, 2) + qt, BF), pltpu.VMEM((2, 4, 2) + qt, BF), pltpu.VMEM((4, 2) + qt, BF),
@@ -763,7 +771,7 @@
         pltpu.VMEM((8,) + vt, F32),
         dma(10), dma(7), dma(7), dma(9, 4), dma(9, 4), dma(4, 4), dma(4, 4), dma(4, 4), dma(4, 4),
         dma(5, 2), dma(5, 2), dma(5, 2), dma(5), dma(5), dma(5),
-        dma(2), dma(2), dma(2), dma(2), dma(2, 7), dma(2, 7),
+        dma(3), dma(3), dma(2), dma(2), dma(2, 7), dma(2, 7),
     ]
     return pl.pallas_call(
         back_kernel,

time: 243 us -> 238 us (0.979)
  Pallas kernels: 236 us -> 233 us
where the time goes in v2:
time: 238 us; the launch traced here: 236 us
  Pallas kernels  233 us (98%)
  local copies, waits for them, and re-layouts  2.43 us (1%)
    pallas_call x1, Pallas kernels, back(): pl.pallas_call(back_kernel, out_shape=[jax.ShapeDtypeStruct((2,) + tok, F...  98.2 us
    pallas_call x1, Pallas kernels, front(): pl.pallas_call(front_kernel, out_shape=[jax.ShapeDtypeStruct((8, span, wi...  92.1 us
    pallas_call x1, Pallas kernels, mid(): pl.pallas_call(mid_kernel, out_shape=[shape((tokens, width), BF), shape((...  39.7 us

profile of v2, /device:TPU:28, one launch (start us, length us, event | category | flops | bytes accessed | tf_op | source)
XLA Modules:
  0.0 236.3 jit_solution(16493783158853395677)
XLA Ops:
  0.6 1.4 stack.35.vs
  2.0 92.1 %front.1 = (bf16[8,256,768]{2,1,0:T(8,128)(2,1)}, f32[8,8,256]{2,1,0:T(8,128)}, bf16[4,4,2,3,8,3072]{5,4,3,2,1,0:T(8,128)(2,1)}, bf16[4,4,2,3,8,768]{5,4,3,2,1,0...) custom-call(bf16[2,256,768]{2,1,0:T(8,128)(2,1)} %x.1, ...), custom_call_target="tpu_custom_call" | custom-call | tf_op jit(solution)/shard_map/front/pallas_call | solution.py:388
  94.2 39.7 %mid.1 = (bf16[512,768]{1,0:T(8,128)(2,1)}, f32[512,768]{1,0:T(8,128)}, bf16[2,768,256]{2,1,0:T(8,128)(2,1)}, bf16[768,3072]{1,0:T(8,128)(2,1)}, bf16[768,768]{1...) custom-call(bf16[512,768]{1,0:T(8,128)(2,1)} %bitcast.50, bf16[2,768,256]{2,1,0:T(8,128)(2,1)} %bitcast.56, ...), custom_call_target="tpu_custom_call" | custom-call | tf_op jit(solution)/shard_map/mid/pallas_call | solution.py:962
  133.9 98.2 %back.1 = (f32[2,256,768]{2,1,0:T(8,128)}, f32[3,8,3072]{2,1,0:T(8,128)}, f32[3,8,768]{2,1,0:T(8,128)}, f32[12,8,768]{2,1,0:T(8,128)}, f32[16,128]{1,0:T(8,128)}, /*index=5*/f32[4,3,8,576]{3,2,1,0:T(8,128)}) custom-call(bf16[8,192,256]{2,1,0:T(8,128)(2,1)} %bitcast.54, bf16[2,2,4,2,3,8,3072]{6,5,4,3,2,1,0:T(8,128)(2,1)} %bitcast.48, ...), custom_call_target="tpu_custom_call" | custom-call | tf_op jit(solution)/shard_map/back/pallas_call | solution.py:776
  232.1 0.0 copy-start
  232.1 3.1 %finish.1 = (f32[2,256,768]{2,1,0:T(8,128)}, f32[3,8,3072]{2,1,0:T(8,128)}, f32[3,8,768]{2,1,0:T(8,128)}, f32[12,8,768]{2,1,0:T(8,128)}, f32[24,2304]{1,0:T(8,128)}) custom-call(f32[2,256,768]{2,1,0:T(8,128)} %get-tuple-element.64.ix, f32[3,8,3072]{2,1,0:T(8,128)} %get-tuple-element.65.oi, f32[3,8,768]{2,1,0:T(8,128)} %get-tuple-element.66.oo, ...), custom_call_target="tpu_custom_call" | custom-call | tf_op jit(solution)/shard_map/finish/pallas_call | solution.py:1002
  235.2 0.0 copy-done
  235.2 0.5 slice_bitcast_fusion.3
  235.7 0.5 slice_bitcast_fusion
Async XLA Ops:
  232.1 3.1 %copy-start = (f32[16,128]{1,0:T(8,128)S(1)}, f32[16,128]{1,0:T(8,128)}, u32[]{:S(2)}) copy-start(f32[16,128]{1,0:T(8,128)} %get-tuple-element.71) | copy-start | bytes 24580

commit v3 on v2

--- a/solution.py
+++ b/solution.py
@@ -365,7 +365,7 @@
         relay(k, True)
 
 
-ORDER_K = (4, 3, 5, 2, 6, 1, 7, 0)
+ORDER_K = (4, 5, 3, 6, 2, 7, 1, 0)
 
 
 def any_spec():
@@ -502,7 +502,7 @@
             zero = jnp.zeros((64, QB), F32)
             ra = jnp.concatenate([do, zero], axis=0).T.astype(BF)
             rb = jnp.concatenate([zero, qkv[0, rows, cols].astype(F32)], axis=0).T.astype(BF)
-            fixed.append((inside, lse[g, pl.ds(i, 1)], ra, rb))
+            fixed.append((inside, lse[g, pl.ds(i, 1)], jnp.concatenate([ra, rb], axis=0)))
 
         def block(j, carry):
             at = pl.ds(pl.multiple_of(j * KB, KB), KB)
@@ -511,11 +511,11 @@
             dp = [jnp.dot(vk[g, at, :], da[i, g * 64:(g + 1) * 64], preferred_element_type=F32)
                   for g in range(NH)]
             for g in range(NH):
-                inside, lse_i, ra, rb = fixed[g]
+                inside, lse_i, rab = fixed[g]
                 p = jnp.exp2(s[g] * SCORE_SCALE - lse_i)
                 ds = (p * (dp[g] - inside)).astype(BF)
-                dkv[g, at, :] += jnp.dot(p.astype(BF), ra, preferred_element_type=F32) + jnp.dot(
-                    ds, rb, preferred_element_type=F32)
+                dkv[g, at, :] += jnp.dot(
+                    jnp.concatenate([p.astype(BF), ds], axis=1), rab, preferred_element_type=F32)
                 out.append(carry[g] + jnp.dot(qkv[1, g * 64:(g + 1) * 64, at], ds, preferred_element_type=F32))
             return tuple(out)
 

time: 238 us -> 237 us (level)
  no operation moved by 1% of the time
where the time goes in v3:
time: 237 us; the launch traced here: 235 us
  Pallas kernels  232 us (98%)
  local copies, waits for them, and re-layouts  2.43 us (1%)
    pallas_call x1, Pallas kernels, back(): pl.pallas_call(back_kernel, out_shape=[jax.ShapeDtypeStruct((2,) + tok, F...  97.9 us
    pallas_call x1, Pallas kernels, front(): pl.pallas_call(front_kernel, out_shape=[jax.ShapeDtypeStruct((8, span, wi...  91.1 us
    pallas_call x1, Pallas kernels, mid(): pl.pallas_call(mid_kernel, out_shape=[shape((tokens, width), BF), shape((...  39.6 us

profile of v3, /device:TPU:28, one launch (start us, length us, event | category | flops | bytes accessed | tf_op | source)
XLA Modules:
  0.0 234.9 jit_solution(8042017458911770816)
XLA Ops:
  0.6 1.4 stack.35.vs
  2.0 91.1 %front.1 = (bf16[8,256,768]{2,1,0:T(8,128)(2,1)}, f32[8,8,256]{2,1,0:T(8,128)}, bf16[4,4,2,3,8,3072]{5,4,3,2,1,0:T(8,128)(2,1)}, bf16[4,4,2,3,8,768]{5,4,3,2,1,0...) custom-call(bf16[2,256,768]{2,1,0:T(8,128)(2,1)} %x.1, ...), custom_call_target="tpu_custom_call" | custom-call | tf_op jit(solution)/shard_map/front/pallas_call | solution.py:388
  93.1 39.6 %mid.1 = (bf16[512,768]{1,0:T(8,128)(2,1)}, f32[512,768]{1,0:T(8,128)}, bf16[2,768,256]{2,1,0:T(8,128)(2,1)}, bf16[768,3072]{1,0:T(8,128)(2,1)}, bf16[768,768]{1...) custom-call(bf16[512,768]{1,0:T(8,128)(2,1)} %bitcast.50, bf16[2,768,256]{2,1,0:T(8,128)(2,1)} %bitcast.56, ...), custom_call_target="tpu_custom_call" | custom-call | tf_op jit(solution)/shard_map/mid/pallas_call | solution.py:962
  132.7 97.9 %back.1 = (f32[2,256,768]{2,1,0:T(8,128)}, f32[3,8,3072]{2,1,0:T(8,128)}, f32[3,8,768]{2,1,0:T(8,128)}, f32[12,8,768]{2,1,0:T(8,128)}, f32[16,128]{1,0:T(8,128)}, /*index=5*/f32[4,3,8,576]{3,2,1,0:T(8,128)}) custom-call(bf16[8,192,256]{2,1,0:T(8,128)(2,1)} %bitcast.54, bf16[2,2,4,2,3,8,3072]{6,5,4,3,2,1,0:T(8,128)(2,1)} %bitcast.48, ...), custom_call_target="tpu_custom_call" | custom-call | tf_op jit(solution)/shard_map/back/pallas_call | solution.py:776
  230.7 0.0 copy-start
  230.7 3.1 %finish.1 = (f32[2,256,768]{2,1,0:T(8,128)}, f32[3,8,3072]{2,1,0:T(8,128)}, f32[3,8,768]{2,1,0:T(8,128)}, f32[12,8,768]{2,1,0:T(8,128)}, f32[24,2304]{1,0:T(8,128)}) custom-call(f32[2,256,768]{2,1,0:T(8,128)} %get-tuple-element.64.ix, f32[3,8,3072]{2,1,0:T(8,128)} %get-tuple-element.65.oi, f32[3,8,768]{2,1,0:T(8,128)} %get-tuple-element.66.oo, ...), custom_call_target="tpu_custom_call" | custom-call | tf_op jit(solution)/shard_map/finish/pallas_call | solution.py:1002
  233.8 0.0 copy-done
  233.8 0.5 slice_bitcast_fusion.3
  234.3 0.5 slice_bitcast_fusion
Async XLA Ops:
  230.7 3.1 %copy-start = (f32[16,128]{1,0:T(8,128)S(1)}, f32[16,128]{1,0:T(8,128)}, u32[]{:S(2)}) copy-start(f32[16,128]{1,0:T(8,128)} %get-tuple-element.71) | copy-start | bytes 24580
